TPU v7x, 512 devices: a whole 4x4x16 slice. The times are simulated.
512 devices in a mesh: fsdp: 32 (over x, z_hi, core), ctx: 16 (over y, z_lo).
Axes of the slice: x: 4, y: 4, z: 16 (z_hi: 4, z_lo: 4; z = z_hi * 4 + z_lo), core: 2. Of those that a mesh axis runs over, the one named last changes fastest.
Arguments:
- features: bfloat16 [3, 16384, 8192], P(None, 'ctx', 'fsdp'), may hold values from -6 to 6
- short_taps: float32 [3, 3, 8192], P(None, None, 'fsdp'), may hold values from -3.5 to 3.5
- decay_rates: float32 [512, 16], P('fsdp'), may hold values from 1.5258789e-05 to 0.1
- mode_gains: float32 [512, 16], P('fsdp'), may hold values from -2.5 to 2.5
- cotangent: bfloat16 [16384, 8192], P('ctx', 'fsdp'), may hold values from -6 to 6
Outputs:
- mixer_output: bfloat16 [16384, 8192], P('ctx', 'fsdp')
- feature_grads: bfloat16 [3, 16384, 8192], P(None, 'ctx', 'fsdp')
- gain_grads: float32 [512, 16], P('fsdp')
- rate_grads: float32 [512, 16], P('fsdp')
All inputs are finite; a program needn't handle non-finite values.
Results may differ from a plain program's by a relative error of at most 0.0048.
Values may be sent and summed in bfloat16 or wider, within the bound.
A program may use at most 64 MiB of HBM per device.

v0:
```python
import jax
import jax.numpy as jnp
from jax import lax
from jax.sharding import PartitionSpec as P

precise = lax.Precision.HIGHEST
threepass = lax.Precision.HIGH


def passed_along(value, axis, steps):
    count = lax.axis_size(axis)
    leading, last = (max(0, -steps), min(count, count - steps))
    return lax.ppermute(value, axis, [(source, source + steps) for source in range(leading, last)])


def diagonal_sums(gram_acc):
    group_count, block_len, width_same = gram_acc.shape
    flipped = jnp.flip(gram_acc, axis=2)
    padded = jnp.concatenate([flipped, jnp.zeros_like(flipped)], axis=2)
    flattened = padded.reshape(group_count, 2 * block_len * block_len)[
        :, : block_len * (2 * block_len - 1)
    ]
    sheared = flattened.reshape(group_count, block_len, 2 * block_len - 1)
    return jnp.sum(sheared, axis=1)[:, block_len - 1 :]


def short_conv(taps_table, row_data, tokens, rim_rows, forward):
    summed = jnp.zeros((3, tokens, row_data.shape[2]), jnp.float32)
    for offset in range(taps_table.shape[1]):
        start_row = rim_rows - offset if forward else offset
        summed = (
            summed + taps_table[:, offset, None, :] * row_data[:, start_row : start_row + tokens, :]
        )
    return summed


def per_device(features, short_taps, decay_rates, mode_gains, cotangent):
    tokens = features.shape[1]
    channels = features.shape[2]
    group_count = decay_rates.shape[0]
    order_count = decay_rates.shape[1]
    members = channels // group_count
    rim_rows = short_taps.shape[1] - 1
    block_len = 128
    block_count = tokens // block_len
    ctx_count = lax.axis_size("ctx")
    ctx_index = lax.axis_index("ctx")
    earlier_rows = passed_along(features[:, tokens - rim_rows :, :], "ctx", 1)
    extended = jnp.concatenate([earlier_rows, features], axis=1)
    shaped = short_conv(short_taps, extended, tokens, rim_rows, True)
    query_part, key_part, value_part = (shaped[0], shaped[1], shaped[2])
    product = (key_part * value_part).astype(jnp.bfloat16)
    adjoint = cotangent * query_part
    grouped_z = product.reshape(tokens, group_count, members)
    grouped_e = adjoint.reshape(tokens, group_count, members)
    mode_coefs = mode_gains * jnp.sqrt(2.0 * decay_rates)
    rate_axis = decay_rates[:, :, None]
    positions = jnp.arange(tokens, dtype=jnp.float32)[None, None, :]
    decay_from = jnp.exp(-rate_axis * positions)
    end_tables = jnp.stack([jnp.flip(decay_from, 2), -jnp.flip(positions * decay_from, 2)])
    end_states = jnp.einsum(
        "kgns,sgm->kngm", end_tables, grouped_z.astype(jnp.float32), precision=threepass
    )
    start_state = jnp.einsum("gnt,tgm->ngm", decay_from, grouped_e, precision=precise)
    local_states = jnp.stack([end_states[0], end_states[1], start_state]).reshape(
        3, order_count, channels
    )
    lag_axis = jnp.arange(block_len, dtype=jnp.float32)[None, None, :]
    block_pow = jnp.exp(-rate_axis * lag_axis)
    block_after = block_pow * jnp.exp(-rate_axis)
    block_moments = jnp.stack([block_after, (lag_axis + 1.0) * block_after])
    coef_after = mode_coefs[:, :, None] * block_after
    block_ends = jnp.stack([jnp.flip(block_pow, 2), -jnp.flip(lag_axis * block_pow, 2)])
    coef_tail = mode_coefs[:, :, None] * jnp.flip(block_after, 2)
    block_span = jnp.exp(-decay_rates * block_len).T[:, :, None]
    lag_index = (
        jnp.arange(block_len, dtype=jnp.int32)[:, None]
        - jnp.arange(block_len, dtype=jnp.int32)[None, :]
    )
    lag_value = jnp.maximum(lag_index, 0).astype(jnp.float32)
    pair_pow = jnp.exp(-decay_rates[:, :, None, None] * lag_value[None, None])
    toeplitz = jnp.where(
        lag_index[None] >= 0, jnp.sum(mode_coefs[:, :, None, None] * pair_pow, axis=1), 0.0
    )
    z_blocks = grouped_z.reshape(block_count, block_len, group_count, members)
    e_blocks = grouped_e.reshape(block_count, block_len, group_count, members)

    def forward_block(carried_in, inputs):
        mode_state, lagged, first_acc, lag_acc, gram_acc = carried_in
        z_block, e_block = inputs
        z_wide = z_block.astype(jnp.float32)
        inside_part = jnp.einsum("gts,sgm->tgm", toeplitz, z_wide, precision=threepass)
        carried = jnp.einsum("gnt,ngm->tgm", coef_after, mode_state, precision=precise)
        moments = jnp.einsum("kgnt,tgm->kngm", block_moments, e_block, precision=precise)
        first_acc = first_acc + jnp.sum(moments[0] * mode_state, axis=2)
        lag_acc = lag_acc + jnp.sum(moments[0] * lagged - moments[1] * mode_state, axis=2)
        gram_acc = gram_acc + jnp.einsum("tgm,sgm->gts", e_block, z_wide, precision=precise)
        fresh_part = jnp.einsum("kgns,sgm->kngm", block_ends, z_wide, precision=threepass)
        new_lagged = block_span * lagged - block_len * block_span * mode_state + fresh_part[1]
        new_state = block_span * mode_state + fresh_part[0]
        return ((new_state, new_lagged, first_acc, lag_acc, gram_acc), inside_part + carried)

    zero_state = jnp.zeros((order_count, group_count, members), jnp.float32)
    zero_pairs = jnp.zeros((order_count, group_count), jnp.float32)
    zero_gram = jnp.zeros((group_count, block_len, block_len), jnp.float32)
    final_carry, inner_blocks = lax.scan(
        forward_block,
        (zero_state, zero_state, zero_pairs, zero_pairs, zero_gram),
        (z_blocks, e_blocks),
    )
    first_acc, lag_acc, gram_acc = (final_carry[2], final_carry[3], final_carry[4])
    lag_totals = diagonal_sums(gram_acc)
    first_local = first_acc.T + jnp.sum(lag_totals[:, None, :] * block_pow, axis=2)
    lag_local = lag_acc.T - jnp.sum(lag_totals[:, None, :] * lag_axis * block_pow, axis=2)
    device_after = decay_from * jnp.exp(-rate_axis)
    second_moment = jnp.einsum(
        "gnt,tgm->ngm", (positions + 1.0) * device_after, grouped_e, precision=precise
    )
    partial_rows = jnp.stack([first_local, lag_local]).reshape(-1, channels)
    partial_slot = jnp.zeros((order_count, channels), jnp.float32)
    partial_slot = partial_slot.at[: partial_rows.shape[0]].set(partial_rows)
    local_states = jnp.concatenate(
        [local_states, second_moment.reshape(1, order_count, channels), partial_slot[None]]
    )
    rate_cols = jnp.repeat(decay_rates.T, members, axis=1)
    everyone = lax.all_gather(local_states[None], "ctx", axis=0, tiled=True)
    device_ids = jnp.arange(ctx_count, dtype=jnp.int32)
    ahead_steps = (ctx_index - 1 - device_ids).astype(jnp.float32)[:, None, None]
    behind_steps = (device_ids - ctx_index - 1).astype(jnp.float32)[:, None, None]
    ahead_weight = jnp.where(
        ahead_steps >= 0, jnp.exp(-rate_cols[None] * (tokens * jnp.maximum(ahead_steps, 0.0))), 0.0
    )
    behind_weight = jnp.where(
        behind_steps >= 0,
        jnp.exp(-rate_cols[None] * (tokens * jnp.maximum(behind_steps, 0.0))),
        0.0,
    )
    prev_state = jnp.sum(ahead_weight * everyone[:, 0], axis=0)
    next_state = jnp.sum(behind_weight * everyone[:, 2], axis=0)
    all_ids = device_ids.astype(jnp.float32)
    pair_steps = (all_ids[:, None] - 1.0 - all_ids[None, :])[:, :, None, None]
    pair_weight = jnp.where(
        pair_steps >= 0,
        jnp.exp(-rate_cols[None, None] * (tokens * jnp.maximum(pair_steps, 0.0))),
        0.0,
    )
    all_prev = jnp.sum(pair_weight * everyone[None, :, 0], axis=1)
    all_lagged = jnp.sum(
        pair_weight * (everyone[None, :, 1] - tokens * pair_steps * everyone[None, :, 0]), axis=1
    )
    all_first = jnp.exp(-rate_cols)[None] * everyone[:, 2]
    cross_first = jnp.sum(all_first * all_prev, axis=0)
    cross_lag = jnp.sum(all_first * all_lagged - everyone[:, 3] * all_prev, axis=0)
    cross_first = cross_first.reshape(order_count, group_count, members).sum(axis=2).T
    cross_lag = cross_lag.reshape(order_count, group_count, members).sum(axis=2).T
    gathered_parts = everyone[:, 4, : partial_rows.shape[0]].reshape(
        ctx_count, 2, group_count, order_count
    )
    local_totals = jnp.sum(gathered_parts, axis=0)
    first_total = local_totals[0] + cross_first
    lag_total = local_totals[1] + cross_lag

    def backward_block(later_state, e_block):
        inside_part = jnp.einsum("gts,tgm->sgm", toeplitz, e_block, precision=precise)
        carried = jnp.einsum("gns,ngm->sgm", coef_tail, later_state, precision=precise)
        fresh_part = jnp.einsum("gnt,tgm->ngm", block_pow, e_block, precision=precise)
        return (block_span * later_state + fresh_part, inside_part + carried)

    top_state, grad_blocks = lax.scan(backward_block, zero_state, e_blocks, reverse=True)
    prev_grouped = prev_state.reshape(order_count, group_count, members)
    next_grouped = next_state.reshape(order_count, group_count, members)
    inner_sum = inner_blocks.reshape(tokens, group_count, members) + jnp.einsum(
        "gnt,ngm->tgm", mode_coefs[:, :, None] * device_after, prev_grouped, precision=precise
    )
    device_tail = mode_coefs[:, :, None] * jnp.flip(device_after, 2)
    product_grad = grad_blocks.reshape(tokens, group_count, members) + jnp.einsum(
        "gns,ngm->sgm", device_tail, next_grouped, precision=precise
    )
    gain_part = jnp.sqrt(2.0 * decay_rates) * first_total
    rate_part = mode_coefs * (0.5 * first_total + decay_rates * lag_total)
    inner_flat = inner_sum.reshape(tokens, channels)
    mixer_output = (query_part * inner_flat).astype(jnp.bfloat16)
    grad_flat = product_grad.reshape(tokens, channels)
    feature_adj = jnp.stack([cotangent * inner_flat, grad_flat * value_part, grad_flat * key_part])
    later_rows = passed_along(feature_adj[:, :rim_rows, :], "ctx", -1)
    appended = jnp.concatenate([feature_adj, later_rows], axis=1)
    feature_grads = short_conv(short_taps, appended, tokens, rim_rows, False).astype(jnp.bfloat16)
    filter_local = jnp.stack([gain_part, rate_part])
    entry_count = 2 * group_count * order_count * lax.axis_size("fsdp")
    summed = filter_local
    squares = lax.psum(jnp.sum(summed * summed), "fsdp")
    factor = jnp.minimum(1.0, lax.rsqrt(squares / entry_count + 1e-06))
    clipped = summed * factor
    return (mixer_output, feature_grads, clipped[0], clipped[1])


def solution(mesh):
    return jax.shard_map(
        per_device,
        mesh=mesh,
        in_specs=(
            P(None, "ctx", "fsdp"),
            P(None, None, "fsdp"),
            P("fsdp", None),
            P("fsdp", None),
            P("ctx", "fsdp"),
        ),
        out_specs=(P("ctx", "fsdp"), P(None, "ctx", "fsdp"), P("fsdp", None), P("fsdp", None)),
        check_vma=False,
    )
```

profile of v0, /device:TPU:1, one launch (start us, length us, event | category | flops | bytes accessed | tf_op | source)
XLA Modules:
  0.0 461.2 jit_solution(7824403788756353742)
XLA Ops:
  8.8 5.1 %collective-permute-start = (bf16[3,2,256]{1,2,0:T(8,128)(2,1)}, bf16[3,2,256]{1,2,0:T(8,128)(2,1)}, u32[]{:S(2)}, u32[]{:S(2)}) collective-permute-start(bf16[3,2,256]{1,2,0:T(8,128)(2,1)} %copy.110), channel_id=1, source_target_pairs={{0,1},{1,2},{2,3},{3,4},{4,5},{5,6},{6,7},{7,8},{8,9},{9,10},{10,1... | collective-permute-start | bytes 9224 | tf_op jit(solution)/shard_map/ppermute | solution.py:13
  28.5 5.2 %multiply_reduce_fusion.1 = f32[16,128,128]{2,1,0:T(8,128)S(1)} fusion(f32[128,128]{1,0:T(8,128)S(1)} %maximum_convert_fusion, f32[16,16]{1,0:T(8,128)S(1)} %get-tuple-element.800, f32[16,16]{1,0:T(8,128)} %copy.115), kind=kLoop, calls=%fused_computation.65 | loop fusion | flops 12320768 | bytes 1116160 | tf_op jit(solution)/shard_map/reduce_sum | solution.py:83
  44.0 5.5 %rev.26 = f32[16,16,1024]{2,1,0:T(8,128)} reverse(f32[16,16,1024]{2,1,0:T(8,128)} %get-tuple-element.565), dimensions={2} | reverse | bytes 2097152 | tf_op jit(solution)/shard_map/jit(_flip)/rev | solution.py:60
  56.4 4.6 %multiply_add_fusion = f32[3,1024,256]{1,2,0:T(8,128)S(1)} fusion(bf16[3,1024,256]{1,2,0:T(8,128)(2,1)} %copy.109, bf16[3,2,256]{1,2,0:T(8,128)(2,1)} %collective-permute-done, f32[3,256]{1,0:T(4,128)} %get-tuple-element.575, f32[3,256]{1,0:T(4,128)} %get-tuple-element.576, f32[3,256]{1,0:T(4,128)} %bitcast.282), kind=kLoop, calls=%fused_computation.76 | loop fusion | flops 11010048 | bytes 4730880 | tf_op jit(solution)/shard_map/add | solution.py:32
  66.1 134.3 %while.39 = (s32[]{:T(128)}, f32[16,16,16]{0,2,1:T(8,128)}, f32[16,16,16]{0,2,1:T(8,128)}, f32[16,16]{0,1:T(8,128)}, f32[16,16]{0,1:T(8,128)}, /*index=5*/f32[16...) while((s32[]{:T(128)}, f32[16,16,16]{0,2,1:T(8,128)}, ...), condition=%wide.region_4.5_spmd.clone, body=%wide.region_1.4_spmd.clone.sunk | while | flops 101380864 | bytes 5014714 | solution.py:106
  74.7 4.5 dynamic_update_slice.17
  91.7 4.5 dynamic_update_slice.17
  108.7 4.5 dynamic_update_slice.17
  125.8 4.5 dynamic_update_slice.17
  142.8 4.5 dynamic_update_slice.17
  159.8 4.5 dynamic_update_slice.17
  176.9 4.5 dynamic_update_slice.17
  193.9 4.5 dynamic_update_slice.17
  200.4 5.8 %rev.28 = f32[16,128,128]{2,1,0:T(8,128)} reverse(f32[16,128,128]{2,1,0:T(8,128)S(1)} %get-tuple-element.253), dimensions={2} | reverse | bytes 2097152 | tf_op jit(solution)/shard_map/jit(_flip)/rev | solution.py:18
  210.3 6.2 %reshape.321 = f32[16,128,255]{2,1,0:T(8,128)} reshape(f32[16,32640]{1,0:T(8,128)} %slice.145) | data formatting | bytes 4177920 | tf_op jit(solution)/shard_map/reshape | solution.py:23
  221.4 5.0 %fusion.63 = f32[2,16,16,16]{1,3,0,2:T(8,128)} fusion(bf16[1024,16,16,1]{0,2,3,1:T(8,128)(2,1)} %bitcast.272, f32[1,16,16,1024]{3,2,0,1:T(8,128)} %negate_bitcast_fusion, f32[1,16,16,1024]{3,2,0,1:T(8,128)} %bitcast.269), kind=kOutput, calls=%fused_computation.91 | convolution fusion | flops 50855936 | bytes 2654208 | tf_op jit(solution)/shard_map/kgns,sgm->kngm/dot_general | solution.py:61
  238.5 48.9 %while.40 = (s32[]{:T(128)}, f32[16,16,16]{0,2,1:T(8,128)S(1)}, f32[8,128,16,16]{1,0,3,2:T(8,128)}, f32[16,16,1]{0,1,2:T(8,128)S(1)}, f32[8,128,16,16]{1,3,2,0:T...) while((s32[]{:T(128)}, f32[16,16,16]{0,2,1:T(8,128)S(1)}, ...), condition=%wide.region_10.11_spmd.clone, body=%wide.region_9.10_spmd.clone.sunk | while | flops 62996484 | bytes 2277520 | solution.py:169
  245.8 4.4 dynamic_update_slice.18
  251.9 4.4 dynamic_update_slice.18
  276.4 4.4 dynamic_update_slice.18
  282.5 4.4 dynamic_update_slice.18
  289.9 30.7 %all-gather.3.cloned.1.call-done = f32[80,16,256]{2,1,0:T(8,128)} async-done(((f32[5,16,256]{2,1,0:T(8,128)}), f32[80,16,256]{2,1,0:T(8,128)}) %all-gather.3.cloned.1.call-update) | async-done | bytes 1310736 | tf_op jit(solution)/shard_map/all_gather | solution.py:126
  329.2 94.6 %psum.7 = f32[]{:T(128)} all-reduce(f32[]{:T(128)} %multiply_reduce_fusion.9), channel_id=1, replica_groups=mesh['fsdp'=32,'ctx'=16] {'fsdp'}, use_global_device_ids=true, to_apply=%region_20.21 | all-reduce | flops 1 | bytes 8 | tf_op jit(solution)/shard_map/psum | solution.py:191
  438.5 8.5 %collective-permute-done.1 = f32[3,2,256]{1,2,0:T(8,128)S(1)} collective-permute-done((f32[3,2,256]{1,2,0:T(8,128)S(1)}, f32[3,2,256]{1,2,0:T(8,128)S(1)}, u32[]{:S(2)}, u32[]{:S(2)}) %collective-permute-start.1) | collective-permute-done | bytes 6176 | tf_op jit(solution)/shard_map/ppermute | solution.py:13
  (283 shorter events, 220.8 us)
Async XLA Ops:
  7.2 17.1 %copy-start.34 = (f32[3,3,256]{2,1,0:T(4,128)S(1)}, f32[3,3,256]{2,1,0:T(4,128)}, u32[]{:S(2)}) copy-start(f32[3,3,256]{2,1,0:T(4,128)} %param.12) | copy-start | bytes 27652
  7.2 17.7 %copy-start.31 = (f32[16,16]{1,0:T(8,128)S(1)}, f32[16,16]{1,0:T(8,128)}, u32[]{:S(2)}) copy-start(f32[16,16]{1,0:T(8,128)} %param.14) | copy-start | bytes 3076
  7.2 313.4 %all-gather.3.cloned.1.call-start = ((), (), s32[]{:S(2)}) async-start(), calls=%async_computation | async-start | bytes 1392640 | tf_op jit(solution)/shard_map/all_gather | solution.py:126
  8.8 47.6 %collective-permute-start = (bf16[3,2,256]{1,2,0:T(8,128)(2,1)}, bf16[3,2,256]{1,2,0:T(8,128)(2,1)}, u32[]{:S(2)}, u32[]{:S(2)}) collective-permute-start(bf16[3,2,256]{1,2,0:T(8,128)(2,1)} %copy.110), channel_id=1, source_target_pairs={{0,1},{1,2},{2,3},{3,4},{4,5},{5,6},{6,7},{7,8},{8,9},{9,10},{10,1... | collective-permute-start | bytes 9224 | tf_op jit(solution)/shard_map/ppermute | solution.py:13
  37.1 12.4 %copy-start.27 = (f32[16,16]{0,1:T(8,128)S(1)}, f32[16,16]{0,1:T(8,128)}, u32[]{:S(2)}) copy-start(f32[16,16]{0,1:T(8,128)} %get-tuple-element.569) | copy-start | bytes 3076
  216.5 13.3 %copy-start.9 = (f32[1024,256]{0,1:T(8,128)S(1)}, f32[1024,256]{0,1:T(8,128)}, u32[]{:S(2)}) copy-start(f32[1024,256]{0,1:T(8,128)} %copy-done.8) | copy-start | bytes 3145732
  287.4 35.3 %copy-start.17 = (f32[16,256]{1,0:T(8,128)S(1)}, f32[16,256]{1,0:T(8,128)}, u32[]{:S(2)}) copy-start(f32[16,256]{1,0:T(8,128)} %neg.43) | copy-start | bytes 49156
  287.4 35.3 %copy-start.32 = (f32[16,16]{1,0:T(8,128)S(1)}, f32[16,16]{1,0:T(8,128)}, u32[]{:S(2)}) copy-start(f32[16,16]{1,0:T(8,128)} %get-tuple-element.573) | copy-start | bytes 3076
  287.4 35.3 %copy-start.33 = (f32[16,16]{1,0:T(8,128)S(1)}, f32[16,16]{1,0:T(8,128)}, u32[]{:S(2)}) copy-start(f32[16,16]{1,0:T(8,128)} %get-tuple-element.574) | copy-start | bytes 3076
  287.4 35.3 %copy-start.39 = (pred[16,16]{1,0:T(8,128)(4,1)S(1)}, pred[16,16]{1,0:T(8,128)(4,1)}, u32[]{:S(2)}) copy-start(pred[16,16]{1,0:T(8,128)(4,1)} %subtract_compare_fusion) | copy-start | bytes 772
  287.4 37.7 %copy-start.22 = (f32[16,256]{1,0:T(8,128)S(1)}, f32[16,256]{1,0:T(8,128)}, u32[]{:S(2)}) copy-start(f32[16,256]{1,0:T(8,128)} %exp.54) | copy-start | bytes 49156
  287.4 37.7 %copy-start.35 = (f32[16]{0:T(128)S(1)}, f32[16]{0:T(128)}, u32[]{:S(2)}) copy-start(f32[16]{0:T(128)} %get-tuple-element.577) | copy-start | bytes 196
  287.4 37.7 %copy-start.36 = (f32[16]{0:T(128)S(1)}, f32[16]{0:T(128)}, u32[]{:S(2)}) copy-start(f32[16]{0:T(128)} %get-tuple-element.578) | copy-start | bytes 196
  287.4 37.7 %copy-start.37 = (pred[16]{0:T(512)(128)(4,1)S(1)}, pred[16]{0:T(512)(128)(4,1)}, u32[]{:S(2)}) copy-start(pred[16]{0:T(512)(128)(4,1)} %get-tuple-element.579) | copy-start | bytes 52
  287.4 37.7 %copy-start.38 = (pred[16]{0:T(512)(128)(4,1)S(1)}, pred[16]{0:T(512)(128)(4,1)}, u32[]{:S(2)}) copy-start(pred[16]{0:T(512)(128)(4,1)} %get-tuple-element.580) | copy-start | bytes 52
  287.5 38.7 %copy-start.19 = (f32[16,16]{0,1:T(8,128)S(1)}, f32[16,16]{0,1:T(8,128)}, u32[]{:S(2)}) copy-start(f32[16,16]{0,1:T(8,128)} %copy-done.18) | copy-start | bytes 3076
  287.5 38.7 %copy-start.21 = (f32[16,16]{0,1:T(8,128)S(1)}, f32[16,16]{0,1:T(8,128)}, u32[]{:S(2)}) copy-start(f32[16,16]{0,1:T(8,128)} %copy-done.20) | copy-start | bytes 3076
  325.4 101.9 %copy-start.1 = (f32[3,1024,256]{1,2,0:T(8,128)S(1)}, f32[3,1024,256]{1,2,0:T(8,128)}, u32[]{:S(2)}) copy-start(f32[3,1024,256]{1,2,0:T(8,128)} %copy-done) | copy-start | bytes 9437188
  433.7 13.3 %copy-start.3 = (f32[1,1024,256]{1,2,0:T(8,128)S(1)}, f32[1,1024,256]{1,2,0:T(8,128)}, u32[]{:S(2)}) copy-start(f32[1,1024,256]{1,2,0:T(8,128)} %get-tuple-element.546) | copy-start | bytes 3145732
  433.7 13.3 %copy-start.5 = (f32[1,1024,256]{1,2,0:T(8,128)S(1)}, f32[1,1024,256]{1,2,0:T(8,128)}, u32[]{:S(2)}) copy-start(f32[1,1024,256]{1,2,0:T(8,128)} %get-tuple-element.547) | copy-start | bytes 3145732
  434.8 12.3 %collective-permute-start.1 = (f32[3,2,256]{1,2,0:T(8,128)S(1)}, f32[3,2,256]{1,2,0:T(8,128)S(1)}, u32[]{:S(2)}, u32[]{:S(2)}) collective-permute-start(f32[3,2,256]{1,2,0:T(8,128)S(1)} %slice.149), channel_id=1, source_target_pairs={{1,0},{2,1},{3,2},{4,3},{5,4},{6,5},{7,6},{8,7},{9,8},{10,9},{11,1... | collective-permute-start | bytes 18440 | tf_op jit(solution)/shard_map/ppermute | solution.py:13
  438.5 10.0 %copy-start.24 = (f32[3,256]{1,0:T(4,128)S(1)}, f32[3,256]{1,0:T(4,128)}, u32[]{:S(2)}) copy-start(f32[3,256]{1,0:T(4,128)} %get-tuple-element.575) | copy-start | bytes 9220
  438.5 10.0 %copy-start.25 = (f32[3,256]{1,0:T(4,128)S(1)}, f32[3,256]{1,0:T(4,128)}, u32[]{:S(2)}) copy-start(f32[3,256]{1,0:T(4,128)} %get-tuple-element.576) | copy-start | bytes 9220
  438.5 10.0 %copy-start.26 = (f32[3,1,256]{2,0,1:T(4,128)S(1)}, f32[3,1,256]{2,0,1:T(4,128)}, u32[]{:S(2)}) copy-start(f32[3,1,256]{2,0,1:T(4,128)} %copy.183) | copy-start | bytes 9220
  (19 other events, 98.3 us)
Sparse Core Ops, SparseCore 0:
  237.5 83.0 all-gather.2
where the time goes:
time: 465 us; the launch traced here: 461 us
  local copies, waits for them, and re-layouts  136 us (29%)
  matrix products  103 us (22%)
  blocking collectives  94.6 us (20%)
  other arithmetic  66.3 us (14%)
  waiting for transfers between devices  39.2 us (8%)
  between operations  15.4 us (3%)
  starting transfers between devices  6.51 us (1%)
    psum x1, blocking collectives, per_device(): squares = lax.psum(jnp.sum(summed * summed), 'fsdp')  94.6 us
    dynamic_update_slice x16, local copies, waits for them, and re-layouts, per_device(): lax.scan(forward_block, (zero_state, zero_state, zero_pairs, zero_pairs,...  71.2 us
    all_gather x1, waiting for transfers between devices, per_device(): everyone = lax.all_gather(local_states[None], 'ctx', axis=0, tiled=True)  30.7 us
    dot_general x8, matrix products, forward_block(): jnp.einsum('kgnt,tgm->kngm', block_moments, e_block, precision=precise)  23.1 us
    unnamed x96, local copies, waits for them, and re-layouts  17.8 us
    dot_general x8, matrix products, forward_block(): jnp.einsum('tgm,sgm->gts', e_block, z_wide, precision=precise)  16.3 us
    dot_general x8, matrix products, forward_block(): jnp.einsum('kgns,sgm->kngm', block_ends, z_wide, precision=threepass)  13.8 us
    reduce_sum x8, other arithmetic, forward_block(): jnp.sum(moments[0] * lagged - moments[1] * mode_state, axis=2)  13.1 us
  transfers between devices with their start and end apart: 3, of which 2 were waited for; matrix products, arithmetic and copies ran while one was open for 21% of the time, Pallas kernels for 0%

commit v1 on v0

--- a/solution.py
+++ b/solution.py
@@ -5,6 +5,18 @@
 
 precise = lax.Precision.HIGHEST
 threepass = lax.Precision.HIGH
+
+
+def do_sheets_by_axis(packet):
+    return jnp.concatenate(
+        jax.lax.all_to_all(
+            jnp.stack([packet for _ in range(jax.lax.axis_size("ctx"))]),
+            axis_name="ctx",
+            split_axis=0,
+            concat_axis=0,
+        ),
+        axis=0,
+    )
 
 
 def passed_along(value, axis, steps):
@@ -123,7 +135,7 @@
         [local_states, second_moment.reshape(1, order_count, channels), partial_slot[None]]
     )
     rate_cols = jnp.repeat(decay_rates.T, members, axis=1)
-    everyone = lax.all_gather(local_states[None], "ctx", axis=0, tiled=True)
+    everyone = do_sheets_by_axis(local_states[None])
     device_ids = jnp.arange(ctx_count, dtype=jnp.int32)
     ahead_steps = (ctx_index - 1 - device_ids).astype(jnp.float32)[:, None, None]
     behind_steps = (device_ids - ctx_index - 1).astype(jnp.float32)[:, None, None]

time: 465 us -> 430 us (0.925)
  the two profiles are of different devices: /device:TPU:1 before, /device:TPU:96 now
where the time goes in v1:
time: 430 us; the launch traced here: 426 us
  local copies, waits for them, and re-layouts  138 us (32%)
  matrix products  103 us (24%)
  blocking collectives  95.5 us (22%)
  other arithmetic  65.7 us (15%)
  starting transfers between devices  13.1 us (3%)
  waiting for transfers between devices  7.89 us (2%)
    psum x1, blocking collectives, per_device(): squares = lax.psum(jnp.sum(summed * summed), 'fsdp')  95.5 us
    dynamic_update_slice x16, local copies, waits for them, and re-layouts, per_device(): lax.scan(forward_block, (zero_state, zero_state, zero_pairs, zero_pairs,...  71.3 us
    dot_general x8, matrix products, forward_block(): jnp.einsum('kgnt,tgm->kngm', block_moments, e_block, precision=precise)  23.1 us
    unnamed x94, local copies, waits for them, and re-layouts  17.8 us
    dot_general x8, matrix products, forward_block(): jnp.einsum('tgm,sgm->gts', e_block, z_wide, precision=precise)  16.3 us
    dot_general x8, matrix products, forward_block(): jnp.einsum('kgns,sgm->kngm', block_ends, z_wide, precision=threepass)  13.8 us
    reduce_sum x8, other arithmetic, forward_block(): jnp.sum(moments[0] * lagged - moments[1] * mode_state, axis=2)  13 us
    dot_general x8, matrix products, forward_block(): jnp.einsum('gts,sgm->tgm', toeplitz, z_wide, precision=threepass)  11.9 us
  transfers between devices with their start and end apart: 3, of which 1 were waited for; matrix products, arithmetic and copies ran while one was open for 23% of the time, Pallas kernels for 0%

profile of v1, /device:TPU:96, one launch (start us, length us, event | category | flops | bytes accessed | tf_op | source)
XLA Modules:
  0.0 426.0 jit_solution(16456087855170264065)
XLA Ops:
  19.7 5.3 %multiply_reduce_fusion.1 = f32[16,128,128]{2,1,0:T(8,128)S(1)} fusion(f32[128,128]{1,0:T(8,128)} %maximum_convert_fusion, f32[16,16]{1,0:T(8,128)S(1)} %get-tuple-element.828, f32[16,16]{1,0:T(8,128)} %copy.132), kind=kLoop, calls=%fused_computation.65 | loop fusion | flops 12320768 | bytes 1116160 | tf_op jit(solution)/shard_map/reduce_sum | solution.py:95
  35.5 5.5 %rev.26 = f32[16,16,1024]{2,1,0:T(8,128)} reverse(f32[16,16,1024]{2,1,0:T(8,128)} %get-tuple-element.593), dimensions={2} | reverse | bytes 2097152 | tf_op jit(solution)/shard_map/jit(_flip)/rev | solution.py:72
  47.8 4.7 %multiply_add_fusion = f32[3,1024,256]{1,2,0:T(8,128)S(1)} fusion(bf16[3,1024,256]{1,2,0:T(8,128)(2,1)} %copy.126, bf16[3,2,256]{1,2,0:T(8,128)(2,1)} %collective-permute-done, f32[3,256]{1,0:T(4,128)} %get-tuple-element.603, f32[3,256]{1,0:T(4,128)} %get-tuple-element.604, f32[3,256]{1,0:T(4,128)} %bitcast.278), kind=kLoop, calls=%fused_computation.76 | loop fusion | flops 11010048 | bytes 4730880 | tf_op jit(solution)/shard_map/add | solution.py:44
  57.6 134.3 %while.39 = (s32[]{:T(128)}, f32[16,16,16]{0,2,1:T(8,128)}, f32[16,16,16]{0,2,1:T(8,128)}, f32[16,16]{0,1:T(8,128)}, f32[16,16]{0,1:T(8,128)}, /*index=5*/f32[16...) while((s32[]{:T(128)}, f32[16,16,16]{0,2,1:T(8,128)}, ...), condition=%wide.region_4.5_spmd.clone, body=%wide.region_1.4_spmd.clone.sunk | while | flops 101380864 | bytes 5014714 | solution.py:118
  66.2 4.5 %dynamic_update_slice.17 = f32[8,128,16,16]{1,0,3,2:T(8,128)} dynamic-update-slice(f32[8,128,16,16]{1,0,3,2:T(8,128)} %get-tuple-element.791, f32[1,128,16,16]{1,0,3,2:T(1,128)S(1)} %bitcast.257, s32[]{:T(128)} %get-tuple-element.785, s32[]{:T(128)} %constant.108.clone.1..sunk, s32[]{:T(128)} %constant.108.clone.1..sunk, s32[]{:T(128)} %constant.108.clone.1..sunk) | dynamic-update-slice | bytes 262148 | tf_op jit(solution)/shard_map/while/body/jit(dynamic_update_index_in_dim)/dynamic_update_slice | solution.py:118
  83.2 4.5 %dynamic_update_slice.17 = f32[8,128,16,16]{1,0,3,2:T(8,128)} dynamic-update-slice(f32[8,128,16,16]{1,0,3,2:T(8,128)} %get-tuple-element.791, f32[1,128,16,16]{1,0,3,2:T(1,128)S(1)} %bitcast.257, s32[]{:T(128)} %get-tuple-element.785, s32[]{:T(128)} %constant.108.clone.1..sunk, s32[]{:T(128)} %constant.108.clone.1..sunk, s32[]{:T(128)} %constant.108.clone.1..sunk) | dynamic-update-slice | bytes 262148 | tf_op jit(solution)/shard_map/while/body/jit(dynamic_update_index_in_dim)/dynamic_update_slice | solution.py:118
  100.3 4.5 %dynamic_update_slice.17 = f32[8,128,16,16]{1,0,3,2:T(8,128)} dynamic-update-slice(f32[8,128,16,16]{1,0,3,2:T(8,128)} %get-tuple-element.791, f32[1,128,16,16]{1,0,3,2:T(1,128)S(1)} %bitcast.257, s32[]{:T(128)} %get-tuple-element.785, s32[]{:T(128)} %constant.108.clone.1..sunk, s32[]{:T(128)} %constant.108.clone.1..sunk, s32[]{:T(128)} %constant.108.clone.1..sunk) | dynamic-update-slice | bytes 262148 | tf_op jit(solution)/shard_map/while/body/jit(dynamic_update_index_in_dim)/dynamic_update_slice | solution.py:118
  117.3 4.5 %dynamic_update_slice.17 = f32[8,128,16,16]{1,0,3,2:T(8,128)} dynamic-update-slice(f32[8,128,16,16]{1,0,3,2:T(8,128)} %get-tuple-element.791, f32[1,128,16,16]{1,0,3,2:T(1,128)S(1)} %bitcast.257, s32[]{:T(128)} %get-tuple-element.785, s32[]{:T(128)} %constant.108.clone.1..sunk, s32[]{:T(128)} %constant.108.clone.1..sunk, s32[]{:T(128)} %constant.108.clone.1..sunk) | dynamic-update-slice | bytes 262148 | tf_op jit(solution)/shard_map/while/body/jit(dynamic_update_index_in_dim)/dynamic_update_slice | solution.py:118
  134.3 4.5 %dynamic_update_slice.17 = f32[8,128,16,16]{1,0,3,2:T(8,128)} dynamic-update-slice(f32[8,128,16,16]{1,0,3,2:T(8,128)} %get-tuple-element.791, f32[1,128,16,16]{1,0,3,2:T(1,128)S(1)} %bitcast.257, s32[]{:T(128)} %get-tuple-element.785, s32[]{:T(128)} %constant.108.clone.1..sunk, s32[]{:T(128)} %constant.108.clone.1..sunk, s32[]{:T(128)} %constant.108.clone.1..sunk) | dynamic-update-slice | bytes 262148 | tf_op jit(solution)/shard_map/while/body/jit(dynamic_update_index_in_dim)/dynamic_update_slice | solution.py:118
  151.3 4.5 %dynamic_update_slice.17 = f32[8,128,16,16]{1,0,3,2:T(8,128)} dynamic-update-slice(f32[8,128,16,16]{1,0,3,2:T(8,128)} %get-tuple-element.791, f32[1,128,16,16]{1,0,3,2:T(1,128)S(1)} %bitcast.257, s32[]{:T(128)} %get-tuple-element.785, s32[]{:T(128)} %constant.108.clone.1..sunk, s32[]{:T(128)} %constant.108.clone.1..sunk, s32[]{:T(128)} %constant.108.clone.1..sunk) | dynamic-update-slice | bytes 262148 | tf_op jit(solution)/shard_map/while/body/jit(dynamic_update_index_in_dim)/dynamic_update_slice | solution.py:118
  168.4 4.5 %dynamic_update_slice.17 = f32[8,128,16,16]{1,0,3,2:T(8,128)} dynamic-update-slice(f32[8,128,16,16]{1,0,3,2:T(8,128)} %get-tuple-element.791, f32[1,128,16,16]{1,0,3,2:T(1,128)S(1)} %bitcast.257, s32[]{:T(128)} %get-tuple-element.785, s32[]{:T(128)} %constant.108.clone.1..sunk, s32[]{:T(128)} %constant.108.clone.1..sunk, s32[]{:T(128)} %constant.108.clone.1..sunk) | dynamic-update-slice | bytes 262148 | tf_op jit(solution)/shard_map/while/body/jit(dynamic_update_index_in_dim)/dynamic_update_slice | solution.py:118
  185.4 4.5 %dynamic_update_slice.17 = f32[8,128,16,16]{1,0,3,2:T(8,128)} dynamic-update-slice(f32[8,128,16,16]{1,0,3,2:T(8,128)} %get-tuple-element.791, f32[1,128,16,16]{1,0,3,2:T(1,128)S(1)} %bitcast.257, s32[]{:T(128)} %get-tuple-element.785, s32[]{:T(128)} %constant.108.clone.1..sunk, s32[]{:T(128)} %constant.108.clone.1..sunk, s32[]{:T(128)} %constant.108.clone.1..sunk) | dynamic-update-slice | bytes 262148 | tf_op jit(solution)/shard_map/while/body/jit(dynamic_update_index_in_dim)/dynamic_update_slice | solution.py:118
  191.9 5.8 %rev.28 = f32[16,128,128]{2,1,0:T(8,128)} reverse(f32[16,128,128]{2,1,0:T(8,128)S(1)} %get-tuple-element.253), dimensions={2} | reverse | bytes 2097152 | tf_op jit(solution)/shard_map/jit(_flip)/rev | solution.py:30
  201.9 6.2 %reshape.326 = f32[16,128,255]{2,1,0:T(8,128)} reshape(f32[16,32640]{1,0:T(8,128)} %slice.145) | data formatting | bytes 4177920 | tf_op jit(solution)/shard_map/reshape | solution.py:35
  212.9 5.0 %fusion.63 = f32[2,16,16,16]{1,3,0,2:T(8,128)} fusion(bf16[1024,16,16,1]{0,2,3,1:T(8,128)(2,1)} %bitcast.271, f32[1,16,16,1024]{3,2,0,1:T(8,128)} %negate_bitcast_fusion, f32[1,16,16,1024]{3,2,0,1:T(8,128)} %bitcast.268), kind=kOutput, calls=%fused_computation.92 | convolution fusion | flops 50855936 | bytes 2654208 | tf_op jit(solution)/shard_map/kgns,sgm->kngm/dot_general | solution.py:73
  229.5 8.5 %all-to-all-start = ((f32[16,1,5,16,256]{4,3,2,1,0:T(8,128)}), f32[16,1,5,16,256]{4,3,2,1,0:T(8,128)}, u32[]{:S(2)}, u32[]{:S(2)}) async-start(f32[16,1,5,16,256]{4,3,2,1,0:T(8,128)} %stack.71), calls=%async_computation | async-start | bytes 2621440 | tf_op jit(solution)/shard_map/all_to_all | solution.py:12
  239.2 48.9 %while.40 = (s32[]{:T(128)}, f32[16,16,16]{0,2,1:T(8,128)S(1)}, f32[8,128,16,16]{1,0,3,2:T(8,128)}, f32[16,16,1]{0,1,2:T(8,128)S(1)}, f32[8,128,16,16]{1,3,2,0:T...) while((s32[]{:T(128)}, f32[16,16,16]{0,2,1:T(8,128)S(1)}, ...), condition=%wide.region_10.11_spmd.clone, body=%wide.region_9.10_spmd.clone.sunk | while | flops 62996484 | bytes 2277520 | solution.py:181
  240.4 4.4 %dynamic_update_slice.18 = f32[8,128,16,16]{1,0,3,2:T(8,128)} dynamic-update-slice(f32[8,128,16,16]{1,0,3,2:T(8,128)} %get-tuple-element.834, f32[1,128,16,16]{1,0,3,2:T(1,128)S(1)} %bitcast.258, s32[]{:T(128)S(6)} %sub.210, s32[]{:T(128)} %constant.108.clone.1..sunk.1, s32[]{:T(128)} %constant.108.clone.1..sunk.1, s32[]{:T(128)} %constant.108.clone.1..sunk.1) | dynamic-update-slice | bytes 262148 | tf_op jit(solution)/shard_map/while/body/jit(dynamic_update_index_in_dim)/dynamic_update_slice | solution.py:118
  246.5 4.4 %dynamic_update_slice.18 = f32[8,128,16,16]{1,0,3,2:T(8,128)} dynamic-update-slice(f32[8,128,16,16]{1,0,3,2:T(8,128)} %get-tuple-element.834, f32[1,128,16,16]{1,0,3,2:T(1,128)S(1)} %bitcast.258, s32[]{:T(128)S(6)} %sub.210, s32[]{:T(128)} %constant.108.clone.1..sunk.1, s32[]{:T(128)} %constant.108.clone.1..sunk.1, s32[]{:T(128)} %constant.108.clone.1..sunk.1) | dynamic-update-slice | bytes 262148 | tf_op jit(solution)/shard_map/while/body/jit(dynamic_update_index_in_dim)/dynamic_update_slice | solution.py:118
  252.7 4.4 %dynamic_update_slice.18 = f32[8,128,16,16]{1,0,3,2:T(8,128)} dynamic-update-slice(f32[8,128,16,16]{1,0,3,2:T(8,128)} %get-tuple-element.834, f32[1,128,16,16]{1,0,3,2:T(1,128)S(1)} %bitcast.258, s32[]{:T(128)S(6)} %sub.210, s32[]{:T(128)} %constant.108.clone.1..sunk.1, s32[]{:T(128)} %constant.108.clone.1..sunk.1, s32[]{:T(128)} %constant.108.clone.1..sunk.1) | dynamic-update-slice | bytes 262148 | tf_op jit(solution)/shard_map/while/body/jit(dynamic_update_index_in_dim)/dynamic_update_slice | solution.py:118
  258.8 4.4 %dynamic_update_slice.18 = f32[8,128,16,16]{1,0,3,2:T(8,128)} dynamic-update-slice(f32[8,128,16,16]{1,0,3,2:T(8,128)} %get-tuple-element.834, f32[1,128,16,16]{1,0,3,2:T(1,128)S(1)} %bitcast.258, s32[]{:T(128)S(6)} %sub.210, s32[]{:T(128)} %constant.108.clone.1..sunk.1, s32[]{:T(128)} %constant.108.clone.1..sunk.1, s32[]{:T(128)} %constant.108.clone.1..sunk.1) | dynamic-update-slice | bytes 262148 | tf_op jit(solution)/shard_map/while/body/jit(dynamic_update_index_in_dim)/dynamic_update_slice | solution.py:118
  264.9 4.4 %dynamic_update_slice.18 = f32[8,128,16,16]{1,0,3,2:T(8,128)} dynamic-update-slice(f32[8,128,16,16]{1,0,3,2:T(8,128)} %get-tuple-element.834, f32[1,128,16,16]{1,0,3,2:T(1,128)S(1)} %bitcast.258, s32[]{:T(128)S(6)} %sub.210, s32[]{:T(128)} %constant.108.clone.1..sunk.1, s32[]{:T(128)} %constant.108.clone.1..sunk.1, s32[]{:T(128)} %constant.108.clone.1..sunk.1) | dynamic-update-slice | bytes 262148 | tf_op jit(solution)/shard_map/while/body/jit(dynamic_update_index_in_dim)/dynamic_update_slice | solution.py:118
  298.4 95.5 %psum.7 = f32[]{:T(128)} all-reduce(f32[]{:T(128)} %multiply_reduce_fusion.9), channel_id=1, replica_groups=mesh['fsdp'=32,'ctx'=16] {'fsdp'}, use_global_device_ids=true, to_apply=%region_20.21 | all-reduce | flops 1 | bytes 8 | tf_op jit(solution)/shard_map/psum | solution.py:203
  410.5 7.9 %collective-permute-done.1 = f32[3,2,256]{1,2,0:T(8,128)} collective-permute-done((f32[3,2,256]{1,2,0:T(8,128)}, f32[3,2,256]{1,2,0:T(8,128)}, u32[]{:S(2)}, u32[]{:S(2)}) %collective-permute-start.1) | collective-permute-done | bytes 6176 | tf_op jit(solution)/shard_map/ppermute | solution.py:25
  (282 shorter events, 221.0 us)
Async XLA Ops:
  0.6 14.8 %copy-start.33 = (f32[3,3,256]{2,1,0:T(4,128)S(1)}, f32[3,3,256]{2,1,0:T(4,128)}, u32[]{:S(2)}) copy-start(f32[3,3,256]{2,1,0:T(4,128)} %param.12) | copy-start | bytes 27652
  0.6 15.4 %copy-start.30 = (f32[16,16]{1,0:T(8,128)S(1)}, f32[16,16]{1,0:T(8,128)}, u32[]{:S(2)}) copy-start(f32[16,16]{1,0:T(8,128)} %param.14) | copy-start | bytes 3076
  2.2 45.6 %collective-permute-start = (bf16[3,2,256]{1,2,0:T(8,128)(2,1)}, bf16[3,2,256]{1,2,0:T(8,128)(2,1)}, u32[]{:S(2)}, u32[]{:S(2)}) collective-permute-start(bf16[3,2,256]{1,2,0:T(8,128)(2,1)} %copy.127), channel_id=1, source_target_pairs={{0,1},{1,2},{2,3},{3,4},{4,5},{5,6},{6,7},{7,8},{8,9},{9,10},{10,1... | collective-permute-start | bytes 9224 | tf_op jit(solution)/shard_map/ppermute | solution.py:25
  6.4 10.4 %copy-start.17 = (f32[16,16]{0,1:T(8,128)}, f32[16,16]{0,1:T(8,128)S(1)}, u32[]{:S(2)}) copy-start(f32[16,16]{0,1:T(8,128)S(1)} %copy.130) | copy-start | bytes 3076
  19.6 6.2 %copy-start.12 = (f32[1,16,16,128]{3,2,1,0:T(8,128)S(1)}, f32[1,16,16,128]{3,2,1,0:T(8,128)}, u32[]{:S(2)}) copy-start(f32[1,16,16,128]{3,2,1,0:T(8,128)} %negate_bitcast_fusion.1) | copy-start | bytes 393220
  19.6 6.2 %copy-start.13 = (f32[16,16,128]{2,1,0:T(8,128)S(1)}, f32[16,16,128]{2,1,0:T(8,128)}, u32[]{:S(2)}) copy-start(f32[16,16,128]{2,1,0:T(8,128)} %rev.24) | copy-start | bytes 393220
  19.6 6.9 %copy-start.14 = (f32[1,16,16,128]{3,2,0,1:T(8,128)S(1)}, f32[1,16,16,128]{3,2,0,1:T(8,128)}, u32[]{:S(2)}) copy-start(f32[1,16,16,128]{3,2,0,1:T(8,128)} %get-tuple-element.586) | copy-start | bytes 393220
  19.6 6.9 %copy-start.15 = (f32[1,16,16,128]{3,2,0,1:T(8,128)S(1)}, f32[1,16,16,128]{3,2,0,1:T(8,128)}, u32[]{:S(2)}) copy-start(f32[1,16,16,128]{3,2,0,1:T(8,128)} %get-tuple-element.587) | copy-start | bytes 393220
  19.7 7.6 %copy-start.28 = (f32[3,1,256]{2,1,0:T(1,128)S(1)}, f32[3,1,256]{2,1,0:T(1,128)}, u32[]{:S(2)}) copy-start(f32[3,1,256]{2,1,0:T(1,128)} %get-tuple-element.589) | copy-start | bytes 9220
  19.7 7.6 %copy-start.29 = (f32[3,1,256]{2,1,0:T(1,128)S(1)}, f32[3,1,256]{2,1,0:T(1,128)}, u32[]{:S(2)}) copy-start(f32[3,1,256]{2,1,0:T(1,128)} %get-tuple-element.590) | copy-start | bytes 9220
  19.7 8.2 %copy-start.22 = (pred[128,128]{1,0:T(8,128)(4,1)S(1)}, pred[128,128]{1,0:T(8,128)(4,1)}, u32[]{:S(2)}) copy-start(pred[128,128]{1,0:T(8,128)(4,1)} %fusion.89) | copy-start | bytes 49156
  26.6 6.2 %copy-start.27 = (f32[3,1,256]{2,1,0:T(1,128)S(1)}, f32[3,1,256]{2,1,0:T(1,128)}, u32[]{:S(2)}) copy-start(f32[3,1,256]{2,1,0:T(1,128)} %get-tuple-element.588) | copy-start | bytes 9220
  28.5 12.4 %copy-start.26 = (f32[16,16]{0,1:T(8,128)S(1)}, f32[16,16]{0,1:T(8,128)}, u32[]{:S(2)}) copy-start(f32[16,16]{0,1:T(8,128)} %get-tuple-element.597) | copy-start | bytes 3076
  208.1 13.3 %copy-start.9 = (f32[1024,256]{0,1:T(8,128)S(1)}, f32[1024,256]{0,1:T(8,128)}, u32[]{:S(2)}) copy-start(f32[1024,256]{0,1:T(8,128)} %copy-done.8) | copy-start | bytes 3145732
  229.5 61.0 %all-to-all-start = ((f32[16,1,5,16,256]{4,3,2,1,0:T(8,128)}), f32[16,1,5,16,256]{4,3,2,1,0:T(8,128)}, u32[]{:S(2)}, u32[]{:S(2)}) async-start(f32[16,1,5,16,256]{4,3,2,1,0:T(8,128)} %stack.71), calls=%async_computation | async-start | bytes 2621440 | tf_op jit(solution)/shard_map/all_to_all | solution.py:12
  294.6 102.7 %copy-start.1 = (f32[3,1024,256]{1,2,0:T(8,128)S(1)}, f32[3,1024,256]{1,2,0:T(8,128)}, u32[]{:S(2)}) copy-start(f32[3,1024,256]{1,2,0:T(8,128)} %copy-done) | copy-start | bytes 9437188
  403.9 5.6 %copy-start.11 = (bf16[1024,256]{0,1:T(8,128)(2,1)S(1)}, bf16[1024,256]{0,1:T(8,128)(2,1)}, u32[]{:S(2)}) copy-start(bf16[1024,256]{0,1:T(8,128)(2,1)} %get-tuple-element.579) | copy-start | bytes 1572868
  403.9 14.5 %copy-start.3 = (f32[1,1024,256]{1,2,0:T(8,128)S(1)}, f32[1,1024,256]{1,2,0:T(8,128)}, u32[]{:S(2)}) copy-start(f32[1,1024,256]{1,2,0:T(8,128)} %get-tuple-element.574) | copy-start | bytes 3145732
  403.9 14.5 %copy-start.5 = (f32[1,1024,256]{1,2,0:T(8,128)S(1)}, f32[1,1024,256]{1,2,0:T(8,128)}, u32[]{:S(2)}) copy-start(f32[1,1024,256]{1,2,0:T(8,128)} %get-tuple-element.575) | copy-start | bytes 3145732
  405.7 12.7 %collective-permute-start.1 = (f32[3,2,256]{1,2,0:T(8,128)}, f32[3,2,256]{1,2,0:T(8,128)}, u32[]{:S(2)}, u32[]{:S(2)}) collective-permute-start(f32[3,2,256]{1,2,0:T(8,128)} %slice.149), channel_id=1, source_target_pairs={{1,0},{2,1},{3,2},{4,3},{5,4},{6,5},{7,6},{8,7},{9,8},{10,9},{11,1... | collective-permute-start | bytes 18440 | tf_op jit(solution)/shard_map/ppermute | solution.py:25
  410.5 9.6 %copy-start.7 = (f32[1,1024,256]{1,2,0:T(8,128)S(1)}, f32[1,1024,256]{1,2,0:T(8,128)}, u32[]{:S(2)}) copy-start(f32[1,1024,256]{1,2,0:T(8,128)} %copy-done.6) | copy-start | bytes 3145732
  410.5 9.6 %copy-start.23 = (f32[3,256]{1,0:T(4,128)S(1)}, f32[3,256]{1,0:T(4,128)}, u32[]{:S(2)}) copy-start(f32[3,256]{1,0:T(4,128)} %get-tuple-element.603) | copy-start | bytes 9220
  410.5 9.6 %copy-start.24 = (f32[3,256]{1,0:T(4,128)S(1)}, f32[3,256]{1,0:T(4,128)}, u32[]{:S(2)}) copy-start(f32[3,256]{1,0:T(4,128)} %get-tuple-element.604) | copy-start | bytes 9220
  410.5 9.6 %copy-start.25 = (f32[3,1,256]{2,0,1:T(4,128)S(1)}, f32[3,1,256]{2,0,1:T(4,128)}, u32[]{:S(2)}) copy-start(f32[3,1,256]{2,0,1:T(4,128)} %copy.197) | copy-start | bytes 9220
  (18 other events, 57.3 us)
